TPU v7x, 256 devices: a whole 4x4x8 slice. The times are simulated.
256 devices in a mesh: tm: 8 (over z_hi, x), space: 32 (over y, z_lo, core).
Axes of the slice: x: 4, y: 4, z: 8 (z_hi: 2, z_lo: 4; z = z_hi * 4 + z_lo), core: 2. Of those that a mesh axis runs over, the one named last changes fastest.
Arguments:
- eof_basis: bfloat16 [262144, 256], P('space'), may hold values from -0.01171875 to 0.01171875
- snapshots: bfloat16 [262144, 512], P('space', 'tm'), may hold values from -6 to 6
- inverse_energy: float32 [256], replicated, may hold values from 0.022097087 to 0.22097087
- eigen_vectors: bfloat16 [256, 512], replicated, may hold values from -0.375 to 0.375
Outputs:
- reduced_operator: float32 [256, 256], replicated
- rebuilt_modes: bfloat16 [512, 262144], P('tm', 'space')
All inputs are finite; a program needn't handle non-finite values.
Results may differ from a plain program's by a relative error of at most 0.0049.
Values may be sent and summed in bfloat16 or wider, within the bound.
A program may use at most 64 MiB of HBM per device.

v0:
```python
import jax
import jax.numpy as jnp
from jax import lax
from jax.sharding import PartitionSpec as P


def passed_along(block, axis, distance):
    devices = range(lax.axis_size(axis))
    route = [(i - distance, i) for i in devices if i - distance in devices]
    return lax.ppermute(block, axis, route)


def per_device(eof_basis, snapshots, inverse_energy, eigen_vectors):
    partial_value = lax.dot_general(
        eof_basis, snapshots, (((0,), (0,)), ((), ())), preferred_element_type=jnp.float32
    )
    coeffs = lax.psum(partial_value, "space")
    previous = passed_along(coeffs[:, -1:], "tm", 1)
    lagged = jnp.concatenate([previous, coeffs[:, :-1]], axis=1)
    scaled = lagged * inverse_energy[:, None]
    local_part = jnp.dot(coeffs, scaled.T, precision=lax.Precision.HIGHEST)
    reduced_operator = lax.psum(local_part, "tm")
    hour_weights = jnp.dot(
        scaled.T, eigen_vectors.astype(jnp.float32), precision=lax.Precision.HIGHEST
    ).astype(jnp.bfloat16)
    rebuilt = lax.psum_scatter(
        lax.dot_general(
            hour_weights, snapshots, (((0,), (1,)), ((), ())), preferred_element_type=jnp.float32
        ),
        "tm",
        scatter_dimension=0,
        tiled=True,
    )
    return (reduced_operator, rebuilt.astype(jnp.bfloat16))


def solution(mesh):
    in_specs = (P("space", None), P("space", "tm"), P(), P())
    out_specs = (P(), P("tm", "space"))
    return jax.shard_map(
        per_device, mesh=mesh, in_specs=in_specs, out_specs=out_specs, check_vma=False
    )
```

profile of v0, /device:TPU:8, one launch (start us, length us, event | category | flops | bytes accessed | tf_op | source)
XLA Modules:
  0.0 729.5 jit_solution(18432330371849172905)
XLA Ops:
  7.2 0.0 copy-start
  7.2 0.0 copy-start.3
  7.2 0.0 copy-start.2
  7.2 0.0 all-reduce.3.cloned.1.call-start
  7.2 1.1 copy-done
  8.4 3.6 fusion.6
  12.0 0.0 all-reduce.3.cloned.1.call-update
  12.0 0.0 reduce-scatter.2.cloned.1.call-start
  12.1 231.5 %all-reduce.3.cloned.1.call-done = f32[256,64]{0,1:T(8,128)} async-done(((f32[256,64]{0,1:T(8,128)}), f32[256,64]{0,1:T(8,128)}) %all-reduce.3.cloned.1.call-update) | async-done | bytes 65552 | tf_op jit(solution)/shard_map/psum | solution.py:17
  243.6 0.7 slice.8
  244.3 3.4 collective-permute-start
  247.7 1.3 collective-permute-done
  249.0 0.0 copy-done.3
  249.0 0.0 copy-done.2
  249.0 1.1 convolution_convert_fusion
  250.1 8.1 %fusion.5 = f32[512,8192]{1,0:T(8,128)} fusion(bf16[64,512]{1,0:T(8,128)(2,1)S(1)} %convolution_convert_fusion, bf16[8192,64]{0,1:T(8,128)(2,1)S(1)} %copy-done), kind=kOutput, calls=%fused_computation.7 | convolution fusion | flops 536870912 | bytes 17891328 | tf_op jit(solution)/shard_map/dot_general | solution.py:27
  258.2 0.0 copy-start.1
  258.2 0.0 reduce-scatter.2.cloned.1.call-update
  258.2 0.0 all-reduce.5.cloned.1.call-start
  258.2 0.8 copy-done.1
  259.0 1.1 fusion
  260.1 0.0 all-reduce.5.cloned.1.call-update
  260.2 339.3 %reduce-scatter.2.cloned.1.call-done = f32[64,8192]{1,0:T(8,128)} async-done(((f32[512,8192]{1,0:T(8,128)}), f32[64,8192]{1,0:T(8,128)}) %reduce-scatter.2.cloned.1.call-update) | async-done | bytes 2097168 | tf_op jit(solution)/shard_map/reduce_scatter | solution.py:26
  599.5 2.7 convert_element_type.8
  602.1 119.2 %all-reduce.5.cloned.1.call-done = f32[256,256]{1,0:T(8,128)} async-done(((f32[256,256]{1,0:T(8,128)}), f32[256,256]{1,0:T(8,128)}) %all-reduce.5.cloned.1.call-update) | async-done | bytes 262160 | tf_op jit(solution)/shard_map/psum | solution.py:22
  721.3 1.7 copy.8
Async XLA Ops:
  7.2 1.2 copy-start
  7.2 241.8 %copy-start.3 = (f32[256]{0:T(256)S(1)}, f32[256]{0:T(256)}, u32[]{:S(2)}) copy-start(f32[256]{0:T(256)} %param.6) | copy-start | bytes 3076
  7.2 241.8 %copy-start.2 = (bf16[256,512]{1,0:T(8,128)(2,1)S(1)}, bf16[256,512]{1,0:T(8,128)(2,1)}, u32[]{:S(2)}) copy-start(bf16[256,512]{1,0:T(8,128)(2,1)} %param.7) | copy-start | bytes 786436
  7.2 236.4 %all-reduce.3.cloned.1.call-start = ((), (), s32[]{:S(2)}) async-start(), calls=%async_computation.1 | async-start | bytes 131072 | tf_op jit(solution)/shard_map/psum | solution.py:17
  12.0 587.4 %reduce-scatter.2.cloned.1.call-start = ((), (), s32[]{:S(2)}) async-start(), calls=%async_computation.3 | async-start | bytes 18874368 | tf_op jit(solution)/shard_map/reduce_scatter | solution.py:26
  244.3 4.7 collective-permute-start
  258.2 0.8 copy-start.1
  258.2 463.1 %all-reduce.5.cloned.1.call-start = ((), (), s32[]{:S(2)}) async-start(), calls=%async_computation.2 | async-start | bytes 524288 | tf_op jit(solution)/shard_map/psum | solution.py:22
Sparse Core Ops, SparseCore 0:
  12.2 231.4 all-reduce.2
  258.3 341.0 reduce-scatter.1
  602.7 118.6 all-reduce.4
where the time goes:
time: 730 us
  waiting for transfers between devices  691 us (95%)
  matrix products  13.9 us (2%)
  between operations  13.8 us (2%)
    reduce_scatter x1, waiting for transfers between devices, per_device(): lax.psum_scatter(lax.dot_general(hour_weights, snapshots, (((0,), (1,)),...  339 us
    psum x1, waiting for transfers between devices, per_device(): coeffs = lax.psum(partial_value, 'space')  232 us
    psum x1, waiting for transfers between devices, per_device(): reduced_operator = lax.psum(local_part, 'tm')  119 us
  transfers between devices with their start and end apart: 4, of which 4 were waited for; matrix products, arithmetic and copies ran while one was open for 1% of the time, Pallas kernels for 0%

commit v1 on v0

--- a/solution.py
+++ b/solution.py
@@ -14,7 +14,7 @@
     partial_value = lax.dot_general(
         eof_basis, snapshots, (((0,), (0,)), ((), ())), preferred_element_type=jnp.float32
     )
-    coeffs = lax.psum(partial_value, "space")
+    coeffs = jnp.sum(lax.all_gather(partial_value, "space"), axis=0)
     previous = passed_along(coeffs[:, -1:], "tm", 1)
     lagged = jnp.concatenate([previous, coeffs[:, :-1]], axis=1)
     scaled = lagged * inverse_energy[:, None]

time: 730 us -> 545 us (0.75)
  waiting for transfers between devices: 691 us -> 506 us
    psum x1 -> x0, waiting for transfers between devices: 232 us -> none  [per_device(): coeffs = lax.psum(partial_value, 'space')]
    all_gather x0 -> x1, waiting for transfers between devices: none -> 62.6 us  [per_device(): coeffs = jnp.sum(lax.all_gather(partial_value, 'space'), axis=0)]
    reduce_scatter x1, waiting for transfers between devices: 339 us -> 323 us  [per_device(): lax.psum_scatter(lax.dot_general(hour_weights, snapshots, (((0,), (1,)),...]
where the time goes in v1:
time: 545 us
  waiting for transfers between devices  506 us (93%)
  between operations  13.8 us (3%)
  matrix products  13.1 us (2%)
    reduce_scatter x1, waiting for transfers between devices, per_device(): lax.psum_scatter(lax.dot_general(hour_weights, snapshots, (((0,), (1,)),...  323 us
    psum x1, waiting for transfers between devices, per_device(): reduced_operator = lax.psum(local_part, 'tm')  119 us
    all_gather x1, waiting for transfers between devices, per_device(): coeffs = jnp.sum(lax.all_gather(partial_value, 'space'), axis=0)  62.6 us
  transfers between devices with their start and end apart: 4, of which 4 were waited for; matrix products, arithmetic and copies ran while one was open for 1% of the time, Pallas kernels for 0%

profile of v1, /device:TPU:8, one launch (start us, length us, event | category | flops | bytes accessed | tf_op | source)
XLA Modules:
  0.0 544.6 jit_solution(10341583326923322360)
XLA Ops:
  7.2 0.0 copy-start
  7.2 0.0 all-gather.3.cloned.1.call-start
  7.2 1.2 copy-done
  8.4 3.6 fusion.6
  12.0 0.0 copy-start.1
  12.0 0.0 copy-start.2
  12.0 0.0 all-gather.3.cloned.1.call-update
  12.0 0.0 reduce-scatter.2.cloned.1.call-start
  12.1 62.6 %all-gather.3.cloned.1.call-done = f32[8192,64]{0,1:T(8,128)} async-done(((f32[256,64]{0,1:T(8,128)}), f32[8192,64]{0,1:T(8,128)}) %all-gather.3.cloned.1.call-update) | async-done | bytes 2097168 | tf_op jit(solution)/shard_map/all_gather | solution.py:17
  74.6 2.2 copy.6
  76.9 0.2 bitcast_reduce_fusion
  77.1 3.4 collective-permute-start
  80.5 1.3 collective-permute-done
  81.8 0.0 copy-done.1
  81.8 0.0 copy-done.2
  81.8 0.3 convolution_convert_fusion
  82.0 8.1 %fusion.5 = f32[512,8192]{1,0:T(8,128)} fusion(bf16[64,512]{1,0:T(8,128)(2,1)S(1)} %convolution_convert_fusion, bf16[8192,64]{0,1:T(8,128)(2,1)S(1)} %copy-done), kind=kOutput, calls=%fused_computation.8 | convolution fusion | flops 536870912 | bytes 17891328 | tf_op jit(solution)/shard_map/dot_general | solution.py:27
  90.1 0.0 reduce-scatter.2.cloned.1.call-update
  90.2 0.0 all-reduce.2.cloned.1.call-start
  90.2 1.1 fusion
  91.3 0.0 all-reduce.2.cloned.1.call-update
  91.4 323.0 %reduce-scatter.2.cloned.1.call-done = f32[64,8192]{1,0:T(8,128)} async-done(((f32[512,8192]{1,0:T(8,128)}), f32[64,8192]{1,0:T(8,128)}) %reduce-scatter.2.cloned.1.call-update) | async-done | bytes 2097168 | tf_op jit(solution)/shard_map/reduce_scatter | solution.py:26
  414.4 2.7 convert_element_type.8
  417.1 119.4 %all-reduce.2.cloned.1.call-done = f32[256,256]{1,0:T(8,128)} async-done(((f32[256,256]{1,0:T(8,128)}), f32[256,256]{1,0:T(8,128)}) %all-reduce.2.cloned.1.call-update) | async-done | bytes 262160 | tf_op jit(solution)/shard_map/psum | solution.py:22
  536.4 1.7 copy.8
  (1 shorter events, 0.0 us)
Async XLA Ops:
  7.2 1.2 copy-start
  7.2 67.5 %all-gather.3.cloned.1.call-start = ((), (), s32[]{:S(2)}) async-start(), calls=%async_computation.3 | async-start | bytes 2162688 | tf_op jit(solution)/shard_map/all_gather | solution.py:17
  12.0 69.8 %copy-start.1 = (bf16[256,512]{1,0:T(8,128)(2,1)S(1)}, bf16[256,512]{1,0:T(8,128)(2,1)}, u32[]{:S(2)}) copy-start(bf16[256,512]{1,0:T(8,128)(2,1)} %param.7) | copy-start | bytes 786436
  12.0 69.8 %copy-start.2 = (f32[256]{0:T(256)S(1)}, f32[256]{0:T(256)}, u32[]{:S(2)}) copy-start(f32[256]{0:T(256)} %param.6) | copy-start | bytes 3076
  12.0 402.4 %reduce-scatter.2.cloned.1.call-start = ((), (), s32[]{:S(2)}) async-start(), calls=%async_computation.2 | async-start | bytes 18874368 | tf_op jit(solution)/shard_map/reduce_scatter | solution.py:26
  77.1 4.7 collective-permute-start
  90.2 446.3 %all-reduce.2.cloned.1.call-start = ((), (), s32[]{:S(2)}) async-start(), calls=%async_computation.1 | async-start | bytes 524288 | tf_op jit(solution)/shard_map/psum | solution.py:22
Sparse Core Ops, SparseCore 0:
  12.2 62.4 all-gather.2
  90.3 324.0 reduce-scatter.1
  417.6 118.7 all-reduce.1
